TPU v7x, 1024 devices: a whole 4x4x32 slice. The times are simulated.
1024 devices in a mesh: tensor: 16 (over y, x_hi, core), fsdp: 32 (over z), dp: 2 (over x_lo).
Axes of the slice: x: 4 (x_hi: 2, x_lo: 2; x = x_hi * 2 + x_lo), y: 4, z: 32, core: 2. Of those that a mesh axis runs over, the one named last changes fastest.
Arguments:
- tokens: bfloat16 [1024, 8192], P(('tensor', 'dp'), 'fsdp'), may hold values from -6 to 6
- gate_weight: bfloat16 [8192, 28672], P('fsdp', 'tensor'), may hold values from -0.0625 to 0.0625
- up_weight: bfloat16 [8192, 28672], P('fsdp', 'tensor'), may hold values from -0.0625 to 0.0625
- down_weight: bfloat16 [28672, 8192], P('tensor', 'fsdp'), may hold values from -0.03125 to 0.03125
- keep_bits: int32 [1024, 512], P(('tensor', 'dp'), 'fsdp'), may hold values from 0 to 65535
Outputs:
- mixed: bfloat16 [1024, 8192], P(('tensor', 'dp'), 'fsdp')
Inputs may be any that keep to these rules, and one draw needn't show every extreme that they name: `keep_bits`: bit j of word c of a row is the keep flag of column 16 c + j of that row; every 16-bit pattern can occur.
All inputs are finite; a program needn't handle non-finite values.
Results may differ from a plain program's by a relative error of at most 0.0049.
Values may be sent and summed in bfloat16 or wider, within the bound.
A program may use at most 32 MiB of HBM per device.

v0:
```python
import jax
import jax.numpy as jnp
from jax import lax
from jax.sharding import PartitionSpec as P


def shards(tokens, gate_weight, up_weight, down_weight, keep_bits):
    gathered = lax.all_gather(tokens, "tensor", axis=0, tiled=True)
    width_dev = down_weight.shape[1]
    units_dev = gate_weight.shape[1]
    gate_part = jnp.dot(gathered, gate_weight, preferred_element_type=jnp.float32)
    up_part = jnp.dot(gathered, up_weight, preferred_element_type=jnp.float32)
    summed = lax.psum_scatter(
        jnp.concatenate([gate_part, up_part], axis=1), "fsdp", scatter_dimension=0, tiled=True
    )
    hidden = (jax.nn.silu(summed[:, :units_dev]) * summed[:, units_dev:]).astype(jnp.bfloat16)
    projected = jnp.dot(
        lax.all_gather(hidden, "fsdp", axis=0, tiled=True),
        down_weight,
        preferred_element_type=jnp.float32,
    )
    mine = lax.psum_scatter(projected, "tensor", scatter_dimension=0, tiled=True)
    shifts = jnp.arange(16, dtype=jnp.int32)
    keep = jnp.right_shift(keep_bits[:, :, None], shifts[None, None, :]) & 1
    keep = keep.reshape(mine.shape[0], width_dev).astype(jnp.float32)
    return (2.0 * keep * mine).astype(jnp.bfloat16)


def solution(mesh):
    return jax.shard_map(
        shards,
        mesh=mesh,
        in_specs=(
            P(("tensor", "dp"), "fsdp"),
            P("fsdp", "tensor"),
            P("fsdp", "tensor"),
            P("tensor", "fsdp"),
            P(("tensor", "dp"), "fsdp"),
        ),
        out_specs=P(("tensor", "dp"), "fsdp"),
        check_vma=False,
    )
```

profile of v0, /device:TPU:1, one launch (start us, length us, event | category | flops | bytes accessed | tf_op | source)
XLA Modules:
  0.0 454.1 jit_solution(5529041843529693952)
XLA Ops:
  6.5 0.0 copy-start
  6.5 0.0 copy-start.1
  6.5 0.0 reduce-scatter.3.cloned.1.call-start
  6.5 34.4 %all_gather.6 = bf16[512,256]{1,0:T(8,128)(2,1)S(1)} all-gather(bf16[32,256]{1,0:T(8,128)(2,1)} %param.5), channel_id=1, replica_groups=mesh['tensor'=16,'fsdp'=32,'dp'=2] {'tensor'}, dimensions={0}, use_global_device_ids=true | all-gather | bytes 278528 | tf_op jit(solution)/shard_map/all_gather | solution.py:8
  41.0 0.0 copy-done
  41.0 0.6 fusion.1
  41.6 0.0 copy-done.1
  41.6 0.6 fusion.2
  42.3 4.0 pad_maximum_fusion
  46.3 0.0 copy-start.3
  46.3 0.0 reduce-scatter.3.cloned.1.call-update
  46.3 0.0 copy-start.2
  46.3 0.0 all-gather.2.cloned.1.call-start
  46.4 126.9 %reduce-scatter.3.cloned.1.call-done = f32[16,3584]{1,0:T(8,128)} async-done(((f32[512,3584]{1,0:T(8,128)}), f32[16,3584]{1,0:T(8,128)}) %reduce-scatter.3.cloned.1.call-update) | async-done | bytes 229392 | tf_op jit(solution)/shard_map/reduce_scatter | solution.py:13
  173.3 1.6 fusion
  175.0 0.0 all-gather.2.cloned.1.call-update
  175.0 0.0 reduce-scatter.5.cloned.1.call-start
  175.0 135.9 %all-gather.2.cloned.1.call-done = bf16[512,1792]{1,0:T(8,128)(2,1)} async-done(((bf16[16,1792]{1,0:T(8,128)(2,1)}), bf16[512,1792]{1,0:T(8,128)(2,1)}) %all-gather.2.cloned.1.call-update) | async-done | bytes 1835024 | tf_op jit(solution)/shard_map/all_gather | solution.py:18
  311.0 0.0 copy-done.3
  311.0 3.0 fusion.3
  313.9 0.0 reduce-scatter.5.cloned.1.call-update
  313.9 0.0 copy-done.2
  314.0 0.1 copy.7
  314.0 0.1 shift_right_arithmetic.23
  314.1 132.0 %reduce-scatter.5.cloned.1.call-done = f32[32,256]{1,0:T(8,128)} async-done(((f32[512,256]{1,0:T(8,128)}), f32[32,256]{1,0:T(8,128)}) %reduce-scatter.5.cloned.1.call-update) | async-done | bytes 32784 | tf_op jit(solution)/shard_map/reduce_scatter | solution.py:22
  446.2 1.4 multiply_convert_fusion
  (2 shorter events, 0.0 us)
Async XLA Ops:
  6.5 34.4 %copy-start = (bf16[256,1792]{1,0:T(8,128)(2,1)S(1)}, bf16[256,1792]{1,0:T(8,128)(2,1)}, u32[]{:S(2)}) copy-start(bf16[256,1792]{1,0:T(8,128)(2,1)} %param.6) | copy-start | bytes 2752516
  6.5 35.1 %copy-start.1 = (bf16[256,1792]{1,0:T(8,128)(2,1)S(1)}, bf16[256,1792]{1,0:T(8,128)(2,1)}, u32[]{:S(2)}) copy-start(bf16[256,1792]{1,0:T(8,128)(2,1)} %param.7) | copy-start | bytes 2752516
  6.5 166.8 %reduce-scatter.3.cloned.1.call-start = ((), (), s32[]{:S(2)}) async-start(), calls=%async_computation.2 | async-start | bytes 7569408 | tf_op jit(solution)/shard_map/reduce_scatter | solution.py:13
  46.3 264.7 %copy-start.3 = (bf16[1792,256]{1,0:T(8,128)(2,1)S(1)}, bf16[1792,256]{1,0:T(8,128)(2,1)}, u32[]{:S(2)}) copy-start(bf16[1792,256]{1,0:T(8,128)(2,1)} %param.8) | copy-start | bytes 2752516
  46.3 267.6 %copy-start.2 = (s32[32,16]{0,1:T(8,128)S(1)}, s32[32,16]{0,1:T(8,128)}, u32[]{:S(2)}) copy-start(s32[32,16]{0,1:T(8,128)} %param.9) | copy-start | bytes 6148
  46.3 264.6 %all-gather.2.cloned.1.call-start = ((), (), s32[]{:S(2)}) async-start(), calls=%async_computation.3 | async-start | bytes 1892352 | tf_op jit(solution)/shard_map/all_gather | solution.py:18
  175.0 271.2 %reduce-scatter.5.cloned.1.call-start = ((), (), s32[]{:S(2)}) async-start(), calls=%async_computation.4 | async-start | bytes 557056 | tf_op jit(solution)/shard_map/reduce_scatter | solution.py:22
Sparse Core Ops, SparseCore 0:
  46.5 126.8 reduce-scatter.2
  176.0 134.9 all-gather.1
  316.7 129.4 reduce-scatter.4
where the time goes:
time: 455 us; the launch traced here: 454 us
  waiting for transfers between devices  395 us (87%)
  blocking collectives  34.4 us (8%)
  between operations  13.1 us (3%)
  other arithmetic  7.02 us (2%)
    all_gather x1, waiting for transfers between devices, shards(): lax.all_gather(hidden, 'fsdp', axis=0, tiled=True)  136 us
    reduce_scatter x1, waiting for transfers between devices, shards(): lax.psum_scatter(projected, 'tensor', scatter_dimension=0, tiled=True)  132 us
    reduce_scatter x1, waiting for transfers between devices, shards(): lax.psum_scatter(jnp.concatenate([gate_part, up_part], axis=1), 'fsdp', s...  127 us
    all_gather x1, blocking collectives, shards(): gathered = lax.all_gather(tokens, 'tensor', axis=0, tiled=True)  34.4 us
  transfers between devices with their start and end apart: 3, of which 3 were waited for; matrix products, arithmetic and copies ran while one was open for 0% of the time, Pallas kernels for 0%

commit v1 on v0

v1 whole, which is shorter than its diff:
```python
import jax
import jax.numpy as jnp
from jax import lax
from jax.experimental import pallas as pl
from jax.experimental.pallas import tpu as pltpu
from jax.sharding import PartitionSpec as P

MESH = pl.DeviceIdType.MESH
BLOCK = 128
SUBS = (4, 4, 3, 3)
SCALE = 2.0**20
UNSCALE = 2.0**-20


def encode(v):
    q = v * SCALE
    q = q * jnp.abs(q)
    return (q * jnp.abs(q)).astype(jnp.bfloat16)


def decode(t):
    t = t.astype(jnp.float32)
    r = jnp.sqrt(jnp.sqrt(jnp.abs(t))) * UNSCALE
    return jnp.where(t < 0, -r, r)


def make_kernel(nt, nz, rows, depth, units, subs):
    ns = len(subs)
    offs = [sum(subs[:j]) for j in range(ns)]
    half = nz // 2
    chunk = nt * rows // nz
    per = nz // nt

    def hops(j, way):
        return half if (j % 2 == 0) == (way == 0) else half - 1

    def kernel(x_hbm, g_hbm, u_hbm, d_hbm, keep_ref, out_ref, *scratch):
        it = iter(scratch)
        xg = next(it)
        w = [next(it) for _ in range(ns)]
        wd = next(it)
        part = [next(it) for _ in range(ns)]
        rs_send = [next(it) for _ in range(ns)]
        rs_recv = [next(it) for _ in range(ns)]
        hg = [next(it) for _ in range(ns)]
        ysend, yrecv = next(it), next(it)
        x_sem, w_sem = next(it), next(it)
        xs_sem, xr_sem = next(it), next(it)
        rss_sem, rsr_sem = next(it), next(it)
        ags_sem, agr_sem = next(it), next(it)
        ys_sem, yr_sem = next(it), next(it)

        t = lax.axis_index("tensor")
        z = lax.axis_index("fsdp")
        ring = (lax.rem(z + 1, nz), lax.rem(z + nz - 1, nz))
        sign = (1, -1)

        def peer(o):
            return lax.rem(t + o, nt)

        x_copy = pltpu.make_async_copy(x_hbm, xg.at[0], x_sem)
        x_copy.start()
        w_copies = []
        for j in range(ns):
            cols = pl.ds(offs[j], subs[j])
            pair = (
                pltpu.make_async_copy(g_hbm.at[:, cols], w[j].at[:, : subs[j]], w_sem.at[2 * j]),
                pltpu.make_async_copy(u_hbm.at[:, cols], w[j].at[:, subs[j] :], w_sem.at[2 * j + 1]),
            )
            for c in pair:
                c.start()
            w_copies.append(pair)
        d_copy = pltpu.make_async_copy(d_hbm, wd, w_sem.at[2 * ns])
        d_copy.start()

        barrier = pltpu.get_barrier_semaphore()
        for way in range(2):
            pl.semaphore_signal(barrier, inc=1, device_id={"fsdp": ring[way]}, device_id_type=MESH)
        for o in range(1, nt):
            pl.semaphore_signal(barrier, inc=1, device_id={"tensor": peer(o)}, device_id_type=MESH)
        pl.semaphore_wait(barrier, nt + 1)

        x_copy.wait()

        def x_send(o):
            return pltpu.make_async_remote_copy(
                src_ref=xg.at[0],
                dst_ref=xg.at[nt - o],
                send_sem=xs_sem.at[o],
                recv_sem=xr_sem.at[nt - o],
                device_id={"tensor": peer(o)},
                device_id_type=MESH,
            )

        for o in range(1, nt):
            x_send(o).start()
        for o in range(1, nt):
            x_send(nt - o).wait_recv()

        def rs_copy(s, j, way):
            return pltpu.make_async_remote_copy(
                src_ref=rs_send[j].at[way, s],
                dst_ref=rs_recv[j].at[way, s],
                send_sem=rss_sem.at[way, s, j],
                recv_sem=rsr_sem.at[way, s, j],
                device_id={"fsdp": ring[way]},
                device_id_type=MESH,
            )

        def dest(s, j, way):
            return lax.rem(z + sign[way] * (hops(j, way) - s) + nz, nz)

        def rs_step(s, j, way):
            v = part[j][dest(s, j, way)]
            if not (isinstance(s, int) and s == 0):
                rs_copy(s - 1, j, way).wait_recv()
                v = v + decode(rs_recv[j][way, s - 1])
            rs_send[j][way, s] = encode(v)
            rs_copy(s, j, way).start()

        tile_rows = 256
        for j in range(ns):
            for c in w_copies[j]:
                c.wait()
            tile_cols = 2 * BLOCK

            def tile(r, _, j=j):
                xb = xg[pl.ds(r * (tile_rows // rows), tile_rows // rows)].reshape(tile_rows, depth)
                for c in range(2 * subs[j] // tile_cols):
                    cols = pl.ds(c * tile_cols, tile_cols)
                    p = jnp.dot(xb, w[j][:, cols], preferred_element_type=jnp.float32)
                    part[j][pl.ds(r * (tile_rows // chunk), tile_rows // chunk), :, cols] = p.reshape(
                        tile_rows // chunk, chunk, tile_cols
                    )
                return 0

            lax.fori_loop(0, nt * rows // tile_rows, tile, 0)
            for way in range(2):
                rs_step(0, j, way)

        def rs_loop(s, _):
            for j in range(ns):
                for way in range(2):
                    rs_step(s, j, way)
            return 0

        lax.fori_loop(1, half - 1, rs_loop, 0)
        for j in range(ns):
            for way in range(2):
                if hops(j, way) == half:
                    rs_step(half - 1, j, way)

        def ag_copy(s, j, way):
            b = lax.rem(z - sign[way] * s + nz, nz)
            return pltpu.make_async_remote_copy(
                src_ref=hg[j].at[b],
                dst_ref=hg[j].at[b],
                send_sem=ags_sem.at[way, s, j],
                recv_sem=agr_sem.at[way, s, j],
                device_id={"fsdp": ring[way]},
                device_id_type=MESH,
            )

        def ag_wait(s, j, way):
            b = lax.rem(z - sign[way] * (s + 1) + nz, nz)
            pltpu.make_async_remote_copy(
                src_ref=hg[j].at[b],
                dst_ref=hg[j].at[b],
                send_sem=ags_sem.at[way, s, j],
                recv_sem=agr_sem.at[way, s, j],
                device_id={"fsdp": ring[way]},
                device_id_type=MESH,
            ).wait_recv()

        for j in range(ns):
            v = part[j][z]
            for way in range(2):
                last = hops(j, way) - 1
                rs_copy(last, j, way).wait_recv()
                v = v + decode(rs_recv[j][way, last])
            gate, up = v[:, : subs[j]], v[:, subs[j] :]
            hg[j][z] = (gate / (1.0 + jnp.exp(-gate)) * up).astype(jnp.bfloat16)
            for way in range(2):
                ag_copy(0, j, way).start()

        d_copy.wait()

        width = out_ref.shape[1]
        words = keep_ref[...]
        nw = words.shape[1]
        hot = (
            lax.broadcasted_iota(jnp.int32, (nw, width), 1) // 16 == lax.broadcasted_iota(jnp.int32, (nw, width), 0)
        ).astype(jnp.bfloat16)
        low = jnp.dot((words & 255).astype(jnp.bfloat16), hot, preferred_element_type=jnp.float32)
        high = jnp.dot((words >> 8).astype(jnp.bfloat16), hot, preferred_element_type=jnp.float32)
        bit = lax.broadcasted_iota(jnp.int32, (rows, width), 1) % 16
        word = low.astype(jnp.int32) + (high.astype(jnp.int32) << 8)
        keep2 = 2.0 * ((word >> bit) & 1).astype(jnp.float32)

        odd = lax.rem(z, 2)
        turn = 1 - 2 * odd
        mid = z // 2

        def y_copy(q):
            return pltpu.make_async_remote_copy(
                src_ref=ysend.at[q],
                dst_ref=yrecv.at[q],
                send_sem=ys_sem.at[q],
                recv_sem=yr_sem.at[q],
                device_id={"tensor": peer(q)},
                device_id_type=MESH,
            )

        def down(k):
            m = k // 2
            q = lax.rem(mid + turn * m * (2 * lax.rem(k, 2) - 1) + nt, nt)
            y = jnp.zeros((rows, width), jnp.float32)
            for j in range(ns):
                h = hg[j][pl.ds(q * per, per)].reshape(rows, subs[j])
                y = y + jnp.dot(h, wd[pl.ds(offs[j], subs[j]), :], preferred_element_type=jnp.float32)

            @pl.when(q == 0)
            def _():
                yrecv[0] = y

            @pl.when(q != 0)
            def _():
                ysend[q] = y
                y_copy(q).start()

        def ag_loop(k, _):
            for j in range(ns):
                for way in range(2):
                    ag_wait(k - 1, j, way)
                    ag_copy(k, j, way).start()
            down(k)
            return 0

        lax.fori_loop(1, half - 1, ag_loop, 0)
        for j in range(ns):
            for way in range(2):
                ag_wait(half - 2, j, way)
                if hops(j, way) == half:
                    ag_copy(half - 1, j, way).start()
        down(half - 1)
        for j in range(ns):
            for way in range(2):
                if hops(j, way) == half:
                    ag_wait(half - 1, j, way)
        down(half)

        for o in range(1, nt):
            x_send(o).wait_send()

        def drain(s, _):
            for j in range(ns):
                for way in range(2):
                    rs_copy(s, j, way).wait_send()
                    ag_copy(s, j, way).wait_send()
            return 0

        lax.fori_loop(0, half - 1, drain, 0)
        for j in range(ns):
            for way in range(2):
                if hops(j, way) == half:
                    rs_copy(half - 1, j, way).wait_send()
                    ag_copy(half - 1, j, way).wait_send()

        total = yrecv[0]
        for q in range(1, nt):
            y_copy(q).wait_recv()
            total = total + yrecv[q]
        out_ref[...] = (keep2 * total).astype(out_ref.dtype)
        for q in range(1, nt):
            y_copy(q).wait_send()

    return kernel


def solution(mesh):
    nt, nz = mesh.shape["tensor"], mesh.shape["fsdp"]

    def step(tokens, gate_weight, up_weight, down_weight, keep_bits):
        rows, depth = tokens.shape
        units = gate_weight.shape[1]
        width = down_weight.shape[1]
        subs = [b * BLOCK for b in SUBS]
        assert sum(subs) == units
        ns = len(subs)
        half, chunk = nz // 2, nt * rows // nz
        bf, f32 = jnp.bfloat16, jnp.float32
        dma = pltpu.SemaphoreType.DMA
        hbm = pl.BlockSpec(memory_space=pl.ANY)
        vmem = pl.BlockSpec(memory_space=pltpu.VMEM)
        return pl.pallas_call(
            make_kernel(nt, nz, rows, depth, units, subs),
            out_shape=jax.ShapeDtypeStruct((rows, width), bf),
            in_specs=[hbm, hbm, hbm, hbm, vmem],
            out_specs=vmem,
            scratch_shapes=[
                pltpu.VMEM((nt, rows, depth), bf),
                *[pltpu.VMEM((depth, 2 * n), bf) for n in subs],
                pltpu.VMEM((units, width), bf),
                *[pltpu.VMEM((nz, chunk, 2 * n), f32) for n in subs],
                *[pltpu.VMEM((2, half, chunk, 2 * n), bf) for n in subs],
                *[pltpu.VMEM((2, half, chunk, 2 * n), bf) for n in subs],
                *[pltpu.VMEM((nz, chunk, n), bf) for n in subs],
                pltpu.VMEM((nt, rows, width), f32),
                pltpu.VMEM((nt, rows, width), f32),
                dma,
                dma((2 * ns + 1,)),
                dma((nt,)),
                dma((nt,)),
                dma((2, half, ns)),
                dma((2, half, ns)),
                dma((2, half, ns)),
                dma((2, half, ns)),
                dma((nt,)),
                dma((nt,)),
            ],
            compiler_params=pltpu.CompilerParams(
                collective_id=0, has_side_effects=True, vmem_limit_bytes=48 * 1024 * 1024
            ),
            name="ffn",
        )(tokens, gate_weight, up_weight, down_weight, keep_bits)

    return jax.shard_map(
        step,
        mesh=mesh,
        in_specs=(
            P(("tensor", "dp"), "fsdp"),
            P("fsdp", "tensor"),
            P("fsdp", "tensor"),
            P("tensor", "fsdp"),
            P(("tensor", "dp"), "fsdp"),
        ),
        out_specs=P(("tensor", "dp"), "fsdp"),
        check_vma=False,
    )
```

time: 455 us -> 148 us (0.33)
  waiting for transfers between devices: 395 us -> 0 us
  Pallas kernels: 0 us -> 143 us
  blocking collectives: 34.4 us -> 0 us
  between operations: 13.1 us -> 0.01 us
  other arithmetic: 7.02 us -> 0 us
  local copies, waits for them, and re-layouts: 0.18 us -> 4.93 us
    reduce_scatter x2 -> x0, waiting for transfers between devices: 259 us -> none  [the longest x1 132 us: shards(): lax.psum_scatter(projected, 'tensor', scatter_dimension=0, tiled=True)]
    pallas_call x0 -> x1, Pallas kernels: none -> 143 us  [step(): pl.pallas_call(make_kernel(nt, nz, rows, depth, units, subs), out_shape=j...]
    all_gather x1 -> x0, waiting for transfers between devices: 136 us -> none  [shards(): lax.all_gather(hidden, 'fsdp', axis=0, tiled=True)]
    all_gather x1 -> x0, blocking collectives: 34.4 us -> none  [shards(): gathered = lax.all_gather(tokens, 'tensor', axis=0, tiled=True)]
    unnamed x8 -> x10, local copies, waits for them, and re-layouts: 0.02 us -> 4.93 us
  transfers between devices with their start and end apart: 3 -> 0, of which waited for: 3 -> 0; matrix products, arithmetic and copies ran while one was open for 0% -> 0% of each run, Pallas kernels for 0% -> 0%
where the time goes in v1:
time: 148 us; the launch traced here: 147 us
  Pallas kernels  143 us (97%)
  local copies, waits for them, and re-layouts  4.93 us (3%)
    pallas_call x1, Pallas kernels, step(): pl.pallas_call(make_kernel(nt, nz, rows, depth, units, subs), out_shape=j...  143 us
    unnamed x10, local copies, waits for them, and re-layouts  4.93 us

profile of v1, /device:TPU:1, one launch (start us, length us, event | category | flops | bytes accessed | tf_op | source)
XLA Modules:
  0.0 147.5 jit_solution(3347663674876645407)
XLA Ops:
  0.0 0.0 copy-start.3
  0.0 0.8 copy.6.keep_ref
  0.8 0.0 copy-done.3
  0.8 0.0 copy-start
  0.8 1.2 copy-done
  2.0 0.0 copy-start.1
  2.0 1.2 copy-done.1
  3.1 0.0 copy-start.2
  3.2 1.2 copy-done.2
  4.3 142.5 %ffn.1 = bf16[32,256]{1,0:T(8,128)(2,1)S(1)} custom-call(bf16[32,256]{1,0:T(8,128)(2,1)S(1)} %copy-done.3, bf16[256,1792]{1,0:T(8,128)(2,1)S(1)} %copy-done, bf16[256,1792]{1,0:T(8,128)(2,1)S(1)} %copy-done.1, bf16[1792,256]{1,0:T(8,128)(2,1)S(1)} %copy-done.2, s32[32,16]{1,0:T(8,128)S(1)} %copy.6.keep_ref), custom_call_target="tpu_custom_call" | custom-call | tf_op jit(solution)/shard_map/ffn/pallas_call | solution.py:295
  146.9 0.6 copy.8
Async XLA Ops:
  0.0 0.8 copy-start.3
  0.8 1.2 copy-start
  2.0 1.2 copy-start.1
  3.1 1.2 copy-start.2
